TPU v7x, 256 devices: a whole 4x4x8 slice. The times are simulated.
256 devices in a mesh: atoms: 32 (over x_lo, z, core), beads: 8 (over x_hi, y).
Axes of the slice: x: 4 (x_hi: 2, x_lo: 2; x = x_hi * 2 + x_lo), y: 4, z: 8, core: 2. Of those that a mesh axis runs over, the one named last changes fastest.
Arguments:
- positions: float32 [32, 3, 4096], P('beads', None, 'atoms'), may hold values from 0 to 1
- velocities: float32 [32, 3, 4096], P('beads', None, 'atoms'), may hold values from -3 to 3
- charges_in: float32 [32, 4096], P('beads', 'atoms'), may hold values from -3 to 3
- species: int32 [4096], P('atoms'), may hold values from 0 to 7
- neighbors: int32 [8, 4096], P(None, 'atoms'), may hold values from -32 to 32
- k_index: int32 [3, 2048], replicated, may hold values from -8 to 8
- kernel: float32 [2048], replicated, may hold values from 0.1 to 1
- chi_table: float32 [8], replicated, may hold values from -2 to 2
- hard_table: float32 [8], replicated, may hold values from 1 to 4
- bond_table: float32 [8], replicated, may hold values from 0.2 to 0.8
- mass_table: float32 [8], replicated, may hold values from 1 to 8
Outputs:
- new_positions: float32 [32, 3, 4096], P('beads', None, 'atoms')
- new_velocities: float32 [32, 3, 4096], P('beads', None, 'atoms')
- charges: float32 [32, 4096], P('beads', 'atoms')
Inputs may be any that keep to these rules, and one draw needn't show every extreme that they name: species index the tables. `neighbors`: neighbour offsets count in atom order, cyclically over 4096 atoms.
All inputs are finite; a program needn't handle non-finite values.
Results may differ from a plain program's by a relative error of at most 0.00021.
Values sent between devices are 32-bit elements; how exact they have to be, the bound alone decides.
A program may use at most 64 MiB of HBM per device.

v0:
```python
import math
import jax
import jax.numpy as jnp
from jax import lax
from jax.sharding import PartitionSpec as P

KVEC = 2048
QITERS = 2
RIM = 32
SPECIES = 8
two_pi = 2.0 * math.pi
ewald_gain = 4.0
mixing = 0.5
spring_rate = 0.5
time_step = 0.05
HIGH = lax.Precision.HIGHEST


def extended(block, sides, width):
    for axis, dim in sides:
        count = lax.axis_size(axis)
        forward = [(i, i + 1) for i in range(count - 1)]
        forward.append((count - 1, 0))
        backward = [(target, source) for source, target in forward]
        low = lax.ppermute(
            lax.slice_in_dim(block, block.shape[dim] - width, None, axis=dim), axis, forward
        )
        high = lax.ppermute(lax.slice_in_dim(block, 0, width, axis=dim), axis, backward)
        block = jnp.concatenate([low, block, high], axis=dim)
    return block


def phase_tables(positions, nblock):
    angle = two_pi * (
        positions[:, 0, :, None] * nblock[0]
        + positions[:, 1, :, None] * nblock[1]
        + positions[:, 2, :, None] * nblock[2]
    )
    return (jnp.cos(angle), jnp.sin(angle))


def unblock(stacked):
    blocks, beads_here, parts, width = stacked.shape
    return stacked.transpose(1, 2, 0, 3).reshape(beads_here, parts, blocks * width)


def to_blocks(pair, blocks):
    beads_here, parts, total = pair.shape
    return pair.reshape(beads_here, parts, blocks, total // blocks).transpose(2, 0, 1, 3)


def local_factors(positions, charge, wave_blocks):

    def local_visit(unused, nblock):
        cosine, sine_part = phase_tables(positions, nblock)
        real_part = jnp.einsum("ba,bak->bk", charge, cosine, precision=HIGH)
        imag_part = jnp.einsum("ba,bak->bk", charge, sine_part, precision=HIGH)
        pair = jnp.stack([real_part, imag_part], 1)
        return (unused, pair)

    unused, stacked = lax.scan(local_visit, None, wave_blocks)
    return unblock(stacked)


def potential_sum(positions, pair, wave_blocks, kernel_blocks):
    coeff_blocks = to_blocks(pair, wave_blocks.shape[0]) * kernel_blocks[:, None, None, :]

    def potential_visit(accum, inputs):
        nblock, cblock = inputs
        cosine, sine_part = phase_tables(positions, nblock)
        accum = accum + jnp.einsum("bak,bk->ba", cosine, cblock[:, 0], precision=HIGH)
        return (accum + jnp.einsum("bak,bk->ba", sine_part, cblock[:, 1], precision=HIGH), None)

    start = jnp.zeros((positions.shape[0], positions.shape[2]), jnp.float32)
    result, unused = lax.scan(potential_visit, start, (wave_blocks, coeff_blocks))
    return result


def force_sum(positions, pair, wave_blocks, kernel_blocks):
    coeff_blocks = to_blocks(pair, wave_blocks.shape[0]) * kernel_blocks[:, None, None, :]

    def force_visit(accum, inputs):
        nblock, cblock = inputs
        cosine, sine_part = phase_tables(positions, nblock)
        mixed = sine_part * cblock[:, 0][:, None, :] - cosine * cblock[:, 1][:, None, :]
        return (accum + jnp.einsum("bak,dk->bda", mixed, nblock, precision=HIGH), None)

    result, unused = lax.scan(
        force_visit, jnp.zeros(positions.shape, jnp.float32), (wave_blocks, coeff_blocks)
    )
    return result


def summed_factors(positions, charge, wave_blocks):
    return lax.psum(local_factors(positions, charge, wave_blocks), "atoms")


def body(
    positions,
    velocities,
    charges_in,
    species,
    neighbors,
    k_index,
    kernel,
    chi_table,
    hard_table,
    bond_table,
    mass_table,
):
    atom_here = positions.shape[2]
    atom_count = atom_here * lax.axis_size("atoms")
    ewald_scale = ewald_gain / math.sqrt(KVEC * atom_count)
    width = min(256, KVEC)
    blocks = KVEC // width
    wave = k_index.astype(jnp.float32)
    wave_blocks = wave.reshape(3, blocks, width).transpose(1, 0, 2)
    kernel_blocks = kernel.reshape(blocks, width)
    onehot = (species[None, :] == jnp.arange(SPECIES, dtype=jnp.int32)[:, None]).astype(jnp.float32)

    def lookup(table):
        return jnp.sum(table[:, None] * onehot, 0)

    electroneg = lookup(chi_table)
    hardness = lookup(hard_table)
    bond_term = lookup(bond_table)
    atom_mass = lookup(mass_table)
    neighbour_index = jnp.arange(atom_here, dtype=jnp.int32)[None, :] + RIM + neighbors
    charge = charges_in
    for rounds in range(QITERS):
        pair = summed_factors(positions, charge, wave_blocks)
        potential = ewald_scale * potential_sum(positions, pair, wave_blocks, kernel_blocks)
        weighted = bond_term[None, :] * charge
        padded = extended(weighted, (("atoms", 1),), RIM)
        neighbour_sum = jnp.sum(padded[:, neighbour_index], 1)
        relaxed = (1.0 - mixing) * charge + mixing * (
            -(electroneg + potential + bond_term * neighbour_sum) / hardness
        )
        charge_sum = lax.psum(jnp.sum(relaxed, 1), "atoms")
        charge = relaxed - (charge_sum / atom_count)[:, None]
    pair = summed_factors(positions, charge, wave_blocks)
    ewald_force = (
        two_pi
        * ewald_scale
        * charge[:, None, :]
        * force_sum(positions, pair, wave_blocks, kernel_blocks)
    )
    padded_beads = extended(positions, (("beads", 0),), 1)
    laplace = 2.0 * positions - padded_beads[:-2] - padded_beads[2:]
    acceleration = ewald_force / atom_mass[None, None, :] - spring_rate * laplace
    new_velocities = velocities + time_step * acceleration
    new_positions = positions + time_step * new_velocities
    return (new_positions, new_velocities, charge)


def solution(mesh):
    return jax.shard_map(
        body,
        mesh=mesh,
        in_specs=(
            P("beads", None, "atoms"),
            P("beads", None, "atoms"),
            P("beads", "atoms"),
            P("atoms"),
            P(None, "atoms"),
            P(),
            P(),
            P(),
            P(),
            P(),
            P(),
        ),
        out_specs=(P("beads", None, "atoms"), P("beads", None, "atoms"), P("beads", "atoms")),
        check_vma=False,
    )
```

profile of v0, /device:TPU:6, one launch (start us, length us, event | category | flops | bytes accessed | tf_op | source)
XLA Modules:
  0.0 944.2 jit_solution(12425092056688733907)
XLA Ops:
  8.2 5.6 collective-permute-start.1
  15.2 40.7 %while.63 = (s32[]{:T(128)}, f32[8,4,2,256]{3,1,2,0:T(4,128)S(1)}, f32[4,3,128]{2,0,1:T(4,128)S(1)}, f32[8,3,256]{2,1,0:T(4,128)S(1)}, f32[4,128]{1,0:T(4,128)S(1)}, /*index=5*/s32[]{:T(128)}, s32[]{:T(128)}, s32[]{}, s32[]{}) while((s32[]{:T(128)}, f32[8,4,2,256]{3,1,2,0:T(4,128)S(1)}, f32[4,3,128]{2,0,1:T(4,128)S(1)}, ...), condition=%wide.region_2.0_spmd, body=%wide.region_1.0_spmd.sunk | while | flops 4720644 | bytes 114821 | solution.py:61
  57.6 2.8 gather_fusion
  60.6 191.0 %all-reduce.4.cloned.1.call-done = f32[4,2,8,256]{3,0,1,2:T(4,128)} async-done(((f32[4,2,8,256]{3,0,1,2:T(4,128)}), f32[4,2,8,256]{3,0,1,2:T(4,128)}) %all-reduce.4.cloned.1.call-update) | async-done | bytes 65552 | tf_op jit(solution)/shard_map/psum | solution.py:95
  252.5 39.9 %while.66 = (s32[]{:T(128)}, f32[4,128]{1,0:T(4,128)S(1)}, f32[4,3,128]{2,0,1:T(4,128)S(1)}, f32[8,3,256]{2,1,0:T(4,128)S(1)}, f32[8,4,2,256]{3,1,2,0:T(4,128)S(1)}, /*index=5*/s32[]{:T(128)}, s32[]{:T(128)}, s32[]{}, s32[]{}) while((s32[]{:T(128)}, f32[4,128]{1,0:T(4,128)S(1)}, f32[4,3,128]{2,0,1:T(4,128)S(1)}, ...), condition=%wide.region_5.6_spmd.clone, body=%wide.region_4.5_spmd.clone.sunk | while | flops 4720133 | bytes 90255 | solution.py:75
  292.5 54.5 %psum.36 = f32[4]{0:T(128)S(1)} all-reduce(f32[4]{0:T(128)S(1)} %get-tuple-element.386), channel_id=1, replica_groups=mesh['atoms'=32,'beads'=8] {'atoms'}, use_global_device_ids=true, to_apply=%region_10.11 | all-reduce | flops 4 | bytes 32 | tf_op jit(solution)/shard_map/psum | solution.py:139
  347.2 3.9 collective-permute-start.3
  351.0 40.7 %while.64 = (s32[]{:T(128)}, f32[8,4,2,256]{3,1,2,0:T(4,128)S(1)}, f32[4,3,128]{2,0,1:T(4,128)S(1)}, f32[8,3,256]{2,1,0:T(4,128)S(1)}, f32[4,128]{1,0:T(4,128)S(1)}, /*index=5*/s32[]{:T(128)}, s32[]{:T(128)}, s32[]{}, s32[]{}) while((s32[]{:T(128)}, f32[8,4,2,256]{3,1,2,0:T(4,128)S(1)}, f32[4,3,128]{2,0,1:T(4,128)S(1)}, ...), condition=%wide.region_12.13_spmd, body=%wide.region_11.12_spmd.sunk | while | flops 4720644 | bytes 114821 | solution.py:61
  392.7 2.8 gather_fusion.1
  395.6 187.4 %all-reduce.6.cloned.1.call-done = f32[4,2,8,256]{3,0,1,2:T(4,128)} async-done(((f32[4,2,8,256]{3,0,1,2:T(4,128)}), f32[4,2,8,256]{3,0,1,2:T(4,128)}) %all-reduce.6.cloned.1.call-update) | async-done | bytes 65552 | tf_op jit(solution)/shard_map/psum | solution.py:95
  583.9 39.9 %while.67 = (s32[]{:T(128)}, f32[4,128]{1,0:T(4,128)S(1)}, f32[4,3,128]{2,0,1:T(4,128)S(1)}, f32[8,3,256]{2,1,0:T(4,128)S(1)}, f32[8,4,2,256]{3,1,2,0:T(4,128)S(1)}, /*index=5*/s32[]{:T(128)}, s32[]{:T(128)}, s32[]{}, s32[]{}) while((s32[]{:T(128)}, f32[4,128]{1,0:T(4,128)S(1)}, f32[4,3,128]{2,0,1:T(4,128)S(1)}, ...), condition=%wide.region_15.16_spmd.clone, body=%wide.region_14.15_spmd.clone.sunk | while | flops 4720133 | bytes 90255 | solution.py:75
  623.9 54.5 %psum.38 = f32[4]{0:T(128)S(1)} all-reduce(f32[4]{0:T(128)S(1)} %get-tuple-element.382), channel_id=1, replica_groups=mesh['atoms'=32,'beads'=8] {'atoms'}, use_global_device_ids=true, to_apply=%region_18.19 | all-reduce | flops 4 | bytes 32 | tf_op jit(solution)/shard_map/psum | solution.py:139
  678.5 40.8 %while.65 = (s32[]{:T(128)}, f32[8,4,2,256]{3,1,2,0:T(4,128)S(1)}, f32[4,3,128]{2,0,1:T(4,128)S(1)}, f32[8,3,256]{2,1,0:T(4,128)S(1)}, f32[4,128]{1,0:T(4,128)S(1)}, /*index=5*/s32[]{:T(128)}, s32[]{:T(128)}, s32[]{}, s32[]{}) while((s32[]{:T(128)}, f32[8,4,2,256]{3,1,2,0:T(4,128)S(1)}, f32[4,3,128]{2,0,1:T(4,128)S(1)}, ...), condition=%wide.region_20.21_spmd, body=%wide.region_19.20_spmd.sunk | while | flops 4720644 | bytes 114821 | solution.py:61
  721.5 4.2 collective-permute-start.5
  725.7 184.5 %all-reduce.8.cloned.1.call-done = f32[4,2,8,256]{3,0,1,2:T(4,128)} async-done(((f32[4,2,8,256]{3,0,1,2:T(4,128)}), f32[4,2,8,256]{3,0,1,2:T(4,128)}) %all-reduce.8.cloned.1.call-update) | async-done | bytes 65552 | tf_op jit(solution)/shard_map/psum | solution.py:95
  911.0 25.9 %while.68 = (s32[]{:T(128)}, f32[4,3,128]{2,1,0:T(4,128)S(1)}, f32[8,3,256]{2,1,0:T(4,128)S(1)}, f32[4,3,128]{2,0,1:T(4,128)S(1)}, f32[8,4,2,256]{3,1,2,0:T(4,128)S(1)}, /*index=5*/s32[]{:T(128)}, s32[]{:T(128)}, s32[]{}, s32[]{}) while((s32[]{:T(128)}, f32[4,3,128]{2,1,0:T(4,128)S(1)}, f32[8,3,256]{2,1,0:T(4,128)S(1)}, ...), condition=%wide.region_23.24_spmd.clone, body=%wide.region_22.23_spmd.clone.sunk | while | flops 5901317 | bytes 87187 | solution.py:88
  911.1 3.1 fusion.210
  914.4 3.1 fusion.210
  917.6 3.1 fusion.210
  920.8 3.1 fusion.210
  924.1 3.1 fusion.210
  927.3 3.1 fusion.210
  930.6 3.1 fusion.210
  933.8 3.1 fusion.210
  (450 shorter events, 211.7 us)
Async XLA Ops:
  7.2 244.4 %all-reduce.4.cloned.1.call-start = ((), (), s32[]{:S(2)}) async-start(), calls=%async_computation | async-start | bytes 131072 | tf_op jit(solution)/shard_map/psum | solution.py:95
  7.2 0.8 copy-start.4
  8.1 49.3 %collective-permute-start = (f32[4,32]{1,0:T(4,128)S(1)}, f32[4,32]{1,0:T(4,128)S(1)}, u32[]{:S(2)}, u32[]{:S(2)}) collective-permute-start(f32[4,32]{1,0:T(4,128)S(1)} %get-tuple-element.430), channel_id=1, source_target_pairs={{0,8},{8,16},{16,24},{24,32},{32,40},{40,48},{48,56},{56,64},{64,7... | collective-permute-start | bytes 1544 | tf_op jit(solution)/shard_map/ppermute | solution.py:25
  8.2 49.3 %collective-permute-start.1 = (f32[4,32]{1,0:T(4,128)S(1)}, f32[4,32]{1,0:T(4,128)S(1)}, u32[]{:S(2)}, u32[]{:S(2)}) collective-permute-start(f32[4,32]{1,0:T(4,128)S(1)} %get-tuple-element.431), channel_id=1, source_target_pairs={{8,0},{16,8},{24,16},{32,24},{40,32},{48,40},{56,48},{64,56},{72,6... | collective-permute-start | bytes 1544 | tf_op jit(solution)/shard_map/ppermute | solution.py:28
  14.6 0.7 copy-start
  56.0 0.6 copy-start.2
  56.0 0.7 copy-start.7
  56.6 526.4 %all-reduce.6.cloned.1.call-start = ((), (), s32[]{:S(2)}) async-start(), calls=%async_computation.1 | async-start | bytes 131072 | tf_op jit(solution)/shard_map/psum | solution.py:95
  56.7 0.7 copy-start.5
  347.2 45.3 %collective-permute-start.2 = (f32[4,32]{1,0:T(4,128)S(1)}, f32[4,32]{1,0:T(4,128)S(1)}, u32[]{:S(2)}, u32[]{:S(2)}) collective-permute-start(f32[4,32]{1,0:T(4,128)S(1)} %get-tuple-element.428), channel_id=1, source_target_pairs={{0,8},{8,16},{16,24},{24,32},{32,40},{40,48},{48,56},{56,64},{64,7... | collective-permute-start | bytes 1544 | tf_op jit(solution)/shard_map/ppermute | solution.py:25
  347.2 45.3 %collective-permute-start.3 = (f32[4,32]{1,0:T(4,128)S(1)}, f32[4,32]{1,0:T(4,128)S(1)}, u32[]{:S(2)}, u32[]{:S(2)}) collective-permute-start(f32[4,32]{1,0:T(4,128)S(1)} %get-tuple-element.429), channel_id=1, source_target_pairs={{8,0},{16,8},{24,16},{32,24},{40,32},{48,40},{56,48},{64,56},{72,6... | collective-permute-start | bytes 1544 | tf_op jit(solution)/shard_map/ppermute | solution.py:28
  391.8 0.6 copy-start.3
  392.4 517.7 %all-reduce.8.cloned.1.call-start = ((), (), s32[]{:S(2)}) async-start(), calls=%async_computation.2 | async-start | bytes 131072 | tf_op jit(solution)/shard_map/psum | solution.py:95
  719.3 0.6 copy-start.8
  719.3 0.6 copy-start.1
  720.0 217.0 %collective-permute-start.4 = (f32[1,3,128]{2,0,1:T(1,128)S(1)}, f32[1,3,128]{2,0,1:T(1,128)S(1)}, u32[]{:S(2)}, u32[]{:S(2)}) collective-permute-start(f32[1,3,128]{2,0,1:T(1,128)S(1)} %get-tuple-element.426), channel_id=1, source_target_pairs={{0,1},{1,2},{2,3},{3,4},{4,5},{5,6},{6,7},{7,0},{8,9},{9,10},{10,1... | collective-permute-start | bytes 4616 | tf_op jit(solution)/shard_map/ppermute | solution.py:25
  721.5 215.5 %collective-permute-start.5 = (f32[1,3,128]{2,0,1:T(1,128)S(1)}, f32[1,3,128]{2,0,1:T(1,128)S(1)}, u32[]{:S(2)}, u32[]{:S(2)}) collective-permute-start(f32[1,3,128]{2,0,1:T(1,128)S(1)} %get-tuple-element.427), channel_id=1, source_target_pairs={{1,0},{2,1},{3,2},{4,3},{5,4},{6,5},{7,6},{0,7},{9,8},{10,9},{11,1... | collective-permute-start | bytes 4616 | tf_op jit(solution)/shard_map/ppermute | solution.py:28
  911.0 26.0 %copy-start.6 = (f32[4,3,128]{2,0,1:T(4,128)S(1)}, f32[4,3,128]{2,0,1:T(4,128)}, u32[]{:S(2)}) copy-start(f32[4,3,128]{2,0,1:T(4,128)} %param.24) | copy-start | bytes 18436
Sparse Core Ops, SparseCore 0:
  56.8 194.7 all-reduce.3
  392.5 190.4 all-reduce.5
  720.1 190.0 all-reduce.7
where the time goes:
time: 945 us; the launch traced here: 944 us
  waiting for transfers between devices  563 us (60%)
  matrix products  223 us (24%)
  blocking collectives  109 us (12%)
  starting transfers between devices  15.4 us (2%)
  between operations  14.1 us (1%)
  local copies, waits for them, and re-layouts  11.7 us (1%)
    psum x3, waiting for transfers between devices, summed_factors(): return lax.psum(local_factors(positions, charge, wave_blocks), 'atoms')  563 us
    psum x2, blocking collectives, body(): charge_sum = lax.psum(jnp.sum(relaxed, 1), 'atoms')  109 us
    dot_general x24, matrix products, local_visit(): imag_part = jnp.einsum('ba,bak->bk', charge, sine_part, precision=HIGH)  59.9 us
    dot_general x24, matrix products, local_visit(): real_part = jnp.einsum('ba,bak->bk', charge, cosine, precision=HIGH)  59.5 us
    dot_general x16, matrix products, potential_visit(): jnp.einsum('bak,bk->ba', sine_part, cblock[:, 1], precision=HIGH)  39.5 us
    dot_general x16, matrix products, potential_visit(): jnp.einsum('bak,bk->ba', cosine, cblock[:, 0], precision=HIGH)  38.8 us
    dot_general x8, matrix products, force_visit(): jnp.einsum('bak,dk->bda', mixed, nblock, precision=HIGH)  25.1 us
  transfers between devices with their start and end apart: 9, of which 3 were waited for; matrix products, arithmetic and copies ran while one was open for 12% of the time, Pallas kernels for 0%

commit v1 on v0

--- a/solution.py
+++ b/solution.py
@@ -92,7 +92,7 @@
 
 
 def summed_factors(positions, charge, wave_blocks):
-    return lax.psum(local_factors(positions, charge, wave_blocks), "atoms")
+    return jnp.sum(lax.all_gather(local_factors(positions, charge, wave_blocks), "atoms"), axis=0)
 
 
 def body(

time: 945 us -> 566 us (0.60)
  waiting for transfers between devices: 563 us -> 164 us
    psum x3 -> x0, waiting for transfers between devices: 563 us -> none  [summed_factors(): return lax.psum(local_factors(positions, charge, wave_blocks), 'atoms')]
    all_gather x0 -> x3, waiting for transfers between devices: none -> 162 us  [summed_factors(): lax.all_gather(local_factors(positions, charge, wave_blocks), 'atoms')]
  transfers between devices with their start and end apart: 9 -> 9, of which waited for: 3 -> 6; matrix products, arithmetic and copies ran while one was open for 12% -> 6% of each run, Pallas kernels for 0% -> 0%
where the time goes in v1:
time: 566 us; the launch traced here: 563 us
  matrix products  230 us (41%)
  waiting for transfers between devices  164 us (29%)
  blocking collectives  111 us (20%)
  local copies, waits for them, and re-layouts  16.3 us (3%)
  starting transfers between devices  15.5 us (3%)
  between operations  14.2 us (3%)
  other arithmetic  9.52 us (2%)
    all_gather x3, waiting for transfers between devices, summed_factors(): lax.all_gather(local_factors(positions, charge, wave_blocks), 'atoms')  162 us
    psum x2, blocking collectives, body(): charge_sum = lax.psum(jnp.sum(relaxed, 1), 'atoms')  111 us
    dot_general x24, matrix products, local_visit(): imag_part = jnp.einsum('ba,bak->bk', charge, sine_part, precision=HIGH)  63.7 us
    dot_general x24, matrix products, local_visit(): real_part = jnp.einsum('ba,bak->bk', charge, cosine, precision=HIGH)  63.3 us
    dot_general x16, matrix products, potential_visit(): jnp.einsum('bak,bk->ba', sine_part, cblock[:, 1], precision=HIGH)  39.5 us
    dot_general x16, matrix products, potential_visit(): jnp.einsum('bak,bk->ba', cosine, cblock[:, 0], precision=HIGH)  38.8 us
    dot_general x8, matrix products, force_visit(): jnp.einsum('bak,dk->bda', mixed, nblock, precision=HIGH)  25.1 us
    ppermute x3, starting transfers between devices, extended(): lax.ppermute(lax.slice_in_dim(block, 0, width, axis=dim), axis, backward)  13.8 us
  transfers between devices with their start and end apart: 9, of which 6 were waited for; matrix products, arithmetic and copies ran while one was open for 6% of the time, Pallas kernels for 0%

profile of v1, /device:TPU:6, one launch (start us, length us, event | category | flops | bytes accessed | tf_op | source)
XLA Modules:
  0.0 563.2 jit_solution(6706045156608518926)
XLA Ops:
  8.1 53.9 %while.63 = (s32[]{:T(128)}, f32[8,4,2,256]{3,2,1,0:T(2,128)S(1)}, f32[4,3,128]{2,0,1:T(4,128)}, f32[8,3,256]{2,1,0:T(4,128)S(1)}, f32[4,128]{1,0:T(4,128)}, /*index=5*/s32[]{:T(128)}, s32[]{:T(128)}, s32[]{}, s32[]{}) while((s32[]{:T(128)}, f32[8,4,2,256]{3,2,1,0:T(2,128)S(1)}, f32[4,3,128]{2,0,1:T(4,128)}, f32[8,3,256]{2,1,0:T(4,128)S(1)}, ...), condition=%wide.region_2.0_spmd, body=%wide.region_1.0_spmd.sunk | while | flops 4720644 | bytes 98437 | solution.py:61
  11.8 3.0 fusion.193
  18.5 3.0 fusion.193
  63.7 5.8 %collective-permute-start.1 = (f32[4,32]{1,0:T(4,128)S(1)}, f32[4,32]{1,0:T(4,128)S(1)}, u32[]{:S(2)}, u32[]{:S(2)}) collective-permute-start(f32[4,32]{1,0:T(4,128)S(1)} %get-tuple-element.479), channel_id=1, source_target_pairs={{8,0},{16,8},{24,16},{32,24},{40,32},{48,40},{56,48},{64,56},{72,6... | collective-permute-start | bytes 1544 | tf_op jit(solution)/shard_map/ppermute | solution.py:28
  73.9 55.8 %all-gather.4.cloned.1.call-done = f32[32,4,2,2048]{3,1,2,0:T(4,128)} async-done(((f32[1,4,2,2048]{3,1,2,0:T(4,128)}), f32[32,4,2,2048]{3,1,2,0:T(4,128)}) %all-gather.4.cloned.1.call-update) | async-done | bytes 2097168 | tf_op jit(solution)/shard_map/all_gather | solution.py:95
  131.7 39.9 %while.66 = (s32[]{:T(128)}, f32[4,128]{1,0:T(4,128)S(1)}, f32[4,3,128]{2,0,1:T(4,128)S(1)}, f32[8,3,256]{2,1,0:T(4,128)S(1)}, f32[8,4,2,256]{3,0,2,1:T(8,128)S(1)}, /*index=5*/s32[]{:T(128)}, s32[]{:T(128)}, s32[]{}, s32[]{}) while((s32[]{:T(128)}, f32[4,128]{1,0:T(4,128)S(1)}, f32[4,3,128]{2,0,1:T(4,128)S(1)}, ...), condition=%wide.region_5.6_spmd.clone, body=%wide.region_4.5_spmd.clone.sunk | while | flops 4720133 | bytes 90255 | solution.py:75
  171.8 55.5 %psum.14 = f32[4]{0:T(128)S(1)} all-reduce(f32[4]{0:T(128)S(1)} %get-tuple-element.434), channel_id=1, replica_groups=mesh['atoms'=32,'beads'=8] {'atoms'}, use_global_device_ids=true, to_apply=%region_10.11 | all-reduce | flops 4 | bytes 32 | tf_op jit(solution)/shard_map/psum | solution.py:139
  227.4 40.7 %while.64 = (s32[]{:T(128)}, f32[8,4,2,256]{3,2,1,0:T(2,128)S(1)}, f32[4,3,128]{2,0,1:T(4,128)S(1)}, f32[8,3,256]{2,1,0:T(4,128)S(1)}, f32[4,128]{1,0:T(4,128)S(1)}, /*index=5*/s32[]{:T(128)}, s32[]{:T(128)}, s32[]{}, s32[]{}) while((s32[]{:T(128)}, f32[8,4,2,256]{3,2,1,0:T(2,128)S(1)}, f32[4,3,128]{2,0,1:T(4,128)S(1)}, ...), condition=%wide.region_12.13_spmd, body=%wide.region_11.12_spmd.sunk | while | flops 4720644 | bytes 98437 | solution.py:61
  269.0 3.8 collective-permute-start.3
  277.2 51.5 %all-gather.6.cloned.1.call-done = f32[32,4,2,2048]{3,1,2,0:T(4,128)} async-done(((f32[1,4,2,2048]{3,1,2,0:T(4,128)}), f32[32,4,2,2048]{3,1,2,0:T(4,128)}) %all-gather.6.cloned.1.call-update) | async-done | bytes 2097168 | tf_op jit(solution)/shard_map/all_gather | solution.py:95
  330.8 40.0 %while.67 = (s32[]{:T(128)}, f32[4,128]{1,0:T(4,128)S(1)}, f32[4,3,128]{2,0,1:T(4,128)S(1)}, f32[8,3,256]{2,1,0:T(4,128)S(1)}, f32[8,4,2,256]{3,0,2,1:T(8,128)S(1)}, /*index=5*/s32[]{:T(128)}, s32[]{:T(128)}, s32[]{}, s32[]{}) while((s32[]{:T(128)}, f32[4,128]{1,0:T(4,128)S(1)}, f32[4,3,128]{2,0,1:T(4,128)S(1)}, ...), condition=%wide.region_15.16_spmd.clone, body=%wide.region_14.15_spmd.clone.sunk | while | flops 4720133 | bytes 90255 | solution.py:75
  370.9 55.5 %psum.15 = f32[4]{0:T(128)S(1)} all-reduce(f32[4]{0:T(128)S(1)} %get-tuple-element.430), channel_id=1, replica_groups=mesh['atoms'=32,'beads'=8] {'atoms'}, use_global_device_ids=true, to_apply=%region_18.19 | all-reduce | flops 4 | bytes 32 | tf_op jit(solution)/shard_map/psum | solution.py:139
  426.5 40.7 %while.65 = (s32[]{:T(128)}, f32[8,4,2,256]{3,2,1,0:T(2,128)S(1)}, f32[4,3,128]{2,0,1:T(4,128)S(1)}, f32[8,3,256]{2,1,0:T(4,128)S(1)}, f32[4,128]{1,0:T(4,128)S(1)}, /*index=5*/s32[]{:T(128)}, s32[]{:T(128)}, s32[]{}, s32[]{}) while((s32[]{:T(128)}, f32[8,4,2,256]{3,2,1,0:T(2,128)S(1)}, f32[4,3,128]{2,0,1:T(4,128)S(1)}, ...), condition=%wide.region_20.21_spmd, body=%wide.region_19.20_spmd.sunk | while | flops 4720644 | bytes 98437 | solution.py:61
  469.5 4.2 collective-permute-start.5
  473.6 54.2 %all-gather.8.cloned.1.call-done = f32[32,4,2,2048]{3,1,2,0:T(4,128)} async-done(((f32[1,4,2,2048]{3,1,2,0:T(4,128)}), f32[32,4,2,2048]{3,1,2,0:T(4,128)}) %all-gather.8.cloned.1.call-update) | async-done | bytes 2097168 | tf_op jit(solution)/shard_map/all_gather | solution.py:95
  529.9 26.1 %while.68 = (s32[]{:T(128)}, f32[4,3,128]{2,1,0:T(4,128)S(1)}, f32[8,3,256]{2,1,0:T(4,128)S(1)}, f32[4,3,128]{2,0,1:T(4,128)S(1)}, f32[8,4,2,256]{3,0,2,1:T(8,128)S(1)}, /*index=5*/s32[]{:T(128)}, s32[]{:T(128)}, s32[]{}, s32[]{}) while((s32[]{:T(128)}, f32[4,3,128]{2,1,0:T(4,128)S(1)}, f32[8,3,256]{2,1,0:T(4,128)S(1)}, ...), condition=%wide.region_23.24_spmd.clone, body=%wide.region_22.23_spmd.clone.sunk | while | flops 5901317 | bytes 103571 | solution.py:88
  530.0 3.1 fusion.222
  533.3 3.1 fusion.222
  536.5 3.1 fusion.222
  539.8 3.1 fusion.222
  543.1 3.1 fusion.222
  546.3 3.1 fusion.222
  549.6 3.1 fusion.222
  552.8 3.1 fusion.222
  (450 shorter events, 229.5 us)
Async XLA Ops:
  7.2 122.5 %all-gather.4.cloned.1.call-start = ((), (), s32[]{:S(2)}) async-start(), calls=%async_computation | async-start | bytes 2162688 | tf_op jit(solution)/shard_map/all_gather | solution.py:95
  8.0 54.8 %copy-start.6 = (f32[8]{0:T(128)S(1)}, f32[8]{0:T(128)}, u32[]{:S(2)}) copy-start(f32[8]{0:T(128)} %param.33) | copy-start | bytes 100
  8.0 54.8 %copy-start.7 = (s32[128]{0:T(128)S(1)}, s32[128]{0:T(128)}, u32[]{:S(2)}) copy-start(s32[128]{0:T(128)} %param.26) | copy-start | bytes 1540
  8.0 54.8 %copy-start.8 = (f32[8]{0:T(128)S(1)}, f32[8]{0:T(128)}, u32[]{:S(2)}) copy-start(f32[8]{0:T(128)} %param.31) | copy-start | bytes 100
  8.0 54.7 %copy-start.9 = (f32[8]{0:T(128)S(1)}, f32[8]{0:T(128)}, u32[]{:S(2)}) copy-start(f32[8]{0:T(128)} %param.32) | copy-start | bytes 100
  8.0 54.7 %copy-start.10 = (f32[8]{0:T(128)S(1)}, f32[8]{0:T(128)}, u32[]{:S(2)}) copy-start(f32[8]{0:T(128)} %param.30) | copy-start | bytes 100
  8.1 61.4 %copy-start.4 = (s32[8,128]{1,0:T(8,128)S(1)}, s32[8,128]{1,0:T(8,128)}, u32[]{:S(2)}) copy-start(s32[8,128]{1,0:T(8,128)} %param.27) | copy-start | bytes 12292
  8.1 61.4 %copy-start.2 = (f32[2048]{0:T(1024)S(1)}, f32[2048]{0:T(1024)}, u32[]{:S(2)}) copy-start(f32[2048]{0:T(1024)} %param.29) | copy-start | bytes 24580
  62.0 69.7 %copy-start = (f32[4,3,128]{2,0,1:T(4,128)S(1)}, f32[4,3,128]{2,0,1:T(4,128)}, u32[]{:S(2)}) copy-start(f32[4,3,128]{2,0,1:T(4,128)} %get-tuple-element.907) | copy-start | bytes 18436
  62.7 266.1 %all-gather.6.cloned.1.call-start = ((), (), s32[]{:S(2)}) async-start(), calls=%async_computation.1 | async-start | bytes 2162688 | tf_op jit(solution)/shard_map/all_gather | solution.py:95
  63.6 6.8 %collective-permute-start = (f32[4,32]{1,0:T(4,128)S(1)}, f32[4,32]{1,0:T(4,128)S(1)}, u32[]{:S(2)}, u32[]{:S(2)}) collective-permute-start(f32[4,32]{1,0:T(4,128)S(1)} %get-tuple-element.478), channel_id=1, source_target_pairs={{0,8},{8,16},{16,24},{24,32},{32,40},{40,48},{48,56},{56,64},{64,7... | collective-permute-start | bytes 1544 | tf_op jit(solution)/shard_map/ppermute | solution.py:25
  63.7 7.1 %collective-permute-start.1 = (f32[4,32]{1,0:T(4,128)S(1)}, f32[4,32]{1,0:T(4,128)S(1)}, u32[]{:S(2)}, u32[]{:S(2)}) collective-permute-start(f32[4,32]{1,0:T(4,128)S(1)} %get-tuple-element.479), channel_id=1, source_target_pairs={{8,0},{16,8},{24,16},{32,24},{40,32},{48,40},{56,48},{64,56},{72,6... | collective-permute-start | bytes 1544 | tf_op jit(solution)/shard_map/ppermute | solution.py:28
  131.7 40.0 %copy-start.1 = (f32[4,128]{1,0:T(4,128)S(1)}, f32[4,128]{1,0:T(4,128)}, u32[]{:S(2)}) copy-start(f32[4,128]{1,0:T(4,128)} %get-tuple-element.928) | copy-start | bytes 6148
  268.8 259.1 %all-gather.8.cloned.1.call-start = ((), (), s32[]{:S(2)}) async-start(), calls=%async_computation.2 | async-start | bytes 2162688 | tf_op jit(solution)/shard_map/all_gather | solution.py:95
  268.9 5.1 collective-permute-start.2
  269.0 5.2 collective-permute-start.3
  467.2 62.7 %copy-start.5 = (f32[4,128]{1,0:T(4,128)}, f32[4,128]{1,0:T(4,128)S(1)}, u32[]{:S(2)}) copy-start(f32[4,128]{1,0:T(4,128)S(1)} %get-tuple-element.933) | copy-start | bytes 6148
  467.9 88.1 %collective-permute-start.4 = (f32[1,3,128]{2,0,1:T(1,128)S(1)}, f32[1,3,128]{2,0,1:T(1,128)S(1)}, u32[]{:S(2)}, u32[]{:S(2)}) collective-permute-start(f32[1,3,128]{2,0,1:T(1,128)S(1)} %get-tuple-element.474), channel_id=1, source_target_pairs={{0,1},{1,2},{2,3},{3,4},{4,5},{5,6},{6,7},{7,0},{8,9},{9,10},{10,1... | collective-permute-start | bytes 4616 | tf_op jit(solution)/shard_map/ppermute | solution.py:25
  469.5 86.6 %collective-permute-start.5 = (f32[1,3,128]{2,0,1:T(1,128)S(1)}, f32[1,3,128]{2,0,1:T(1,128)S(1)}, u32[]{:S(2)}, u32[]{:S(2)}) collective-permute-start(f32[1,3,128]{2,0,1:T(1,128)S(1)} %get-tuple-element.475), channel_id=1, source_target_pairs={{1,0},{2,1},{3,2},{4,3},{5,4},{6,5},{7,6},{0,7},{9,8},{10,9},{11,1... | collective-permute-start | bytes 4616 | tf_op jit(solution)/shard_map/ppermute | solution.py:28
  529.9 26.1 %copy-start.3 = (f32[4,3,128]{2,0,1:T(4,128)S(1)}, f32[4,3,128]{2,0,1:T(4,128)}, u32[]{:S(2)}) copy-start(f32[4,3,128]{2,0,1:T(4,128)} %param.24) | copy-start | bytes 18436
Sparse Core Ops, SparseCore 0:
  62.8 66.8 all-gather.3
  268.9 59.8 all-gather.5
  468.0 59.8 all-gather.7
